TPU v7x, 32 devices: a whole 2x2x4 slice. The times are simulated.
32 devices in a mesh: ctx: 8 (over y, x, core), mp: 4 (over z).
Axes of the slice: x: 2, y: 2, z: 4, core: 2. Of those that a mesh axis runs over, the one named last changes fastest.
Arguments:
- resid_in: bfloat16 [4096, 8192], P('ctx', 'mp'), may hold values from -6 to 6
- q_mr: bfloat16 [4096, 8192], P('ctx', 'mp'), may hold values from -6 to 6
- k_mr: bfloat16 [4096, 8192], P('ctx', 'mp'), may hold values from -6 to 6
- v_mr: bfloat16 [4096, 8192], P('ctx', 'mp'), may hold values from -6 to 6
- mr_filter: float32 [128, 8192], P(None, 'mp'), may hold values from -0.5 to 0.5
- mr_out: bfloat16 [8192, 8192], P('ctx', 'mp'), may hold values from -0.0625 to 0.0625
- q_li: bfloat16 [4096, 8192], P('ctx', 'mp'), may hold values from -6 to 6
- k_li: bfloat16 [4096, 8192], P('ctx', 'mp'), may hold values from -6 to 6
- li_rate: float32 [8192], P('mp'), may hold values from 2.4414063e-05 to 0.0333333333
- li_residue: float32 [8192], P('mp'), may hold values from 0.5 to 2
Outputs:
- mixed: bfloat16 [4096, 8192], P('ctx', 'mp')
- long_out: bfloat16 [4096, 8192], P('ctx', 'mp')
All inputs are finite; a program needn't handle non-finite values.
Results may differ from a plain program's by a relative error of at most 0.008.
Values may be sent and summed in bfloat16 or wider, within the bound.
A program may use at most 192 MiB of HBM per device.

v0:
```python
import jax
import jax.numpy as jnp
from jax import lax
from jax.sharding import PartitionSpec as P


def passed_along(value, axis, by):
    peers = lax.axis_size(axis)
    pairs = [(i, i + by) for i in range(peers) if 0 <= i + by < peers]
    return lax.ppermute(value, axis, pairs)


def carried_in(value, axis, join, neutral):
    count, mine = (lax.axis_size(axis), lax.axis_index(axis))
    pieces = jax.tree.map(lambda part: lax.all_gather(part, axis), value)
    subtotal = jax.tree.map(
        lambda part, zero: jnp.full_like(part, 0) + jnp.asarray(zero, part.dtype), value, neutral
    )

    def step(position, subtotal):
        longer = join(subtotal, jax.tree.map(lambda part: part[position], pieces))
        return jax.tree.map(lambda new, old: jnp.where(position < mine, new, old), longer, subtotal)

    return lax.fori_loop(0, count - 1, step, subtotal)


def link_pair(earlier, later):
    return (earlier[0] * later[0], later[0] * earlier[1] + later[1])


def body(resid_in, q_mr, k_mr, v_mr, mr_filter, mr_out, q_li, k_li, li_rate, li_residue):
    row_count = q_mr.shape[0]
    chan_count = q_mr.shape[1]
    tap_count = mr_filter.shape[0]
    drive_mr = (k_mr.astype(jnp.float32) * v_mr.astype(jnp.float32)).astype(jnp.bfloat16)
    prev_rows = passed_along(drive_mr[row_count - (tap_count - 1) :], "ctx", 1)
    padded = jnp.concatenate([prev_rows, drive_mr], 0).astype(jnp.float32)[None]
    kernel = mr_filter[::-1][:, None, :]
    filtered = lax.conv_general_dilated(
        padded,
        kernel,
        (1,),
        "VALID",
        dimension_numbers=("NWC", "WIO", "NWC"),
        feature_group_count=chan_count,
        precision=lax.Precision.HIGHEST,
    )[0]
    gated = (q_mr.astype(jnp.float32) * filtered).astype(jnp.bfloat16)
    gathered = lax.all_gather(gated, "mp", axis=1, tiled=True)
    all_rows = lax.all_gather(mr_out, "ctx", axis=0, tiled=True)
    summed = jnp.dot(gathered, all_rows, preferred_element_type=jnp.float32)
    mixed = (resid_in.astype(jnp.float32) + summed).astype(jnp.bfloat16)
    decay = jnp.exp(-li_rate)
    drive_li = k_li.astype(jnp.float32) * mixed.astype(jnp.float32)
    decay_rows = jnp.broadcast_to(decay[None, :], drive_li.shape)
    _, local_state = lax.associative_scan(link_pair, (decay_rows, drive_li), axis=0)
    offsets = jnp.arange(1, row_count + 1, dtype=jnp.float32)[:, None]
    powers = jnp.exp(-li_rate[None, :] * offsets)
    block_end = local_state[row_count - 1]
    block_decay = jnp.exp(-li_rate * row_count)
    identity = (jnp.ones_like(block_decay), jnp.zeros_like(block_end))
    prefix = carried_in((block_decay, block_end), "ctx", link_pair, identity)
    carried = prefix[1]
    state = local_state + powers * carried[None, :]
    scale = li_residue * jnp.sqrt(-jnp.expm1(-2.0 * li_rate))
    long_out = (q_li.astype(jnp.float32) * scale * state).astype(jnp.bfloat16)
    return (mixed, long_out)


def solution(mesh):
    in_specs = (
        P("ctx", "mp"),
        P("ctx", "mp"),
        P("ctx", "mp"),
        P("ctx", "mp"),
        P(None, "mp"),
        P("ctx", "mp"),
        P("ctx", "mp"),
        P("ctx", "mp"),
        P("mp"),
        P("mp"),
    )
    out_specs = (P("ctx", "mp"), P("ctx", "mp"))
    return jax.shard_map(body, mesh=mesh, in_specs=in_specs, out_specs=out_specs, check_vma=False)
```

profile of v0, /device:TPU:0, one launch (start us, length us, event | category | flops | bytes accessed | tf_op | source)
XLA Modules:
  0.0 563.9 jit_solution(2799196935869276048)
XLA Ops:
  7.2 3.1 multiply_convert_fusion.1
  11.2 3.2 collective-permute-start
  14.4 5.2 rev.3
  21.4 45.6 %fusion = f32[1,512,2048]{2,0,1:T(1,128)S(1)} fusion(bf16[1,639,2048]{2,1,0:T(8,128)(2,1)S(1)} %maximum_bitcast_fusion, f32[128,1,2048]{2,0,1:T(8,128)S(1)} %bitcast.22), kind=kOutput, calls=%fused_computation.3 | convolution fusion | flops 1610612736 | bytes 7860224 | tf_op jit(solution)/shard_map/conv_general_dilated | solution.py:39
  67.0 2.9 fusion.2
  71.4 14.1 %all-gather = f32[16384]{0:T(1024)S(1)} all-gather(f32[2048]{0:T(1024)S(1)} %get-tuple-element.139), channel_id=2, replica_groups=mesh['ctx'=8,'mp'=4] {'ctx'}, dimensions={0}, use_global_device_ids=true | all-gather | bytes 73728 | tf_op jit(solution)/shard_map/all_gather | solution.py:15
  86.8 138.0 %all-gather.5.cloned.1.call-done = bf16[512,8192]{1,0:T(8,128)(2,1)} async-done(((bf16[512,2048]{1,0:T(8,128)(2,1)}), bf16[512,8192]{1,0:T(8,128)(2,1)}) %all-gather.5.cloned.1.call-update) | async-done | bytes 8388624 | tf_op jit(solution)/shard_map/all_gather | solution.py:49
  224.8 160.9 %all-gather.7.cloned.1.call-done = bf16[8192,2048]{1,0:T(8,128)(2,1)} async-done(((bf16[1024,2048]{1,0:T(8,128)(2,1)}), bf16[8192,2048]{1,0:T(8,128)(2,1)}) %all-gather.7.cloned.1.call-update) | async-done | bytes 33554448 | tf_op jit(solution)/shard_map/all_gather | solution.py:50
  385.6 25.6 %convert_multiply_fusion = (f32[512,2048]{1,0:T(8,128)}, bf16[512,2048]{1,0:T(8,128)(2,1)}) fusion(bf16[512,2048]{1,0:T(8,128)(2,1)} %param.19, bf16[512,8192]{1,0:T(8,128)(2,1)} %all-gather.5.cloned.1.call-done, bf16[8192,2048]{1,0:T(8,128)(2,1)} %all-gather.7.cloned.1.call-done, bf16[512,2048]{1,0:T(8,128)(2,1)} %param.12), kind=kOutput, calls=%fused_computation.8 | convolution fusion | flops 17186160640 | bytes 52428800 | tf_op jit(solution)/shard_map/dot_general | solution.py:51
  411.3 10.0 %slice.254 = f32[255,2048]{1,0:T(8,128)} slice(f32[512,2048]{1,0:T(8,128)} %get-tuple-element.143), slice={[2:512:2], [0:2048:1]} | slice | bytes 4177920 | tf_op jit(solution)/shard_map/slice | solution.py:56
  421.3 9.8 %slice.200 = f32[256,2048]{1,0:T(8,128)} slice(f32[512,2048]{1,0:T(8,128)} %get-tuple-element.143), slice={[1:512:2], [0:2048:1]} | slice | bytes 4194304 | tf_op jit(solution)/shard_map/slice | solution.py:56
  431.1 9.8 %slice.199 = f32[256,2048]{1,0:T(8,128)} slice(f32[512,2048]{1,0:T(8,128)} %get-tuple-element.143), slice={[0:511:2], [0:2048:1]} | slice | bytes 4194304 | tf_op jit(solution)/shard_map/slice | solution.py:56
  440.9 2.6 multiply_add_fusion
  443.5 2.9 slice.205
  446.4 2.8 slice.204
  479.6 3.0 slice.252
  491.3 4.2 pad.70
  497.4 4.9 pad.69
  502.3 3.4 add.183
  507.9 16.7 %pad.71 = f32[512,2048]{1,0:T(8,128)} pad(f32[256,2048]{1,0:T(8,128)} %pad_maximum_fusion, f32[]{:T(128)} %constant.35.clone.1), padding=0_1_1x0_0_0 | pad | bytes 6291460 | tf_op jit(solution)/shard_map/pad | solution.py:56
  524.7 9.1 %pad.72 = f32[512,2048]{1,0:T(8,128)} pad(f32[256,2048]{1,0:T(8,128)S(1)} %copy-done.3, f32[]{:T(128)} %constant.35.clone.1), padding=1_0_1x0_0_0 | pad | bytes 6291460 | tf_op jit(solution)/shard_map/pad | solution.py:56
  534.6 9.2 %all-gather.1 = f32[8,1,2048]{2,1,0:T(1,128)S(1)} all-gather(f32[1,1,2048]{2,1,0:T(1,128)S(1)} %add_bitcast_fusion), channel_id=1, replica_groups=mesh['ctx'=8,'mp'=4] {'ctx'}, dimensions={0}, use_global_device_ids=true | all-gather | bytes 73728 | tf_op jit(solution)/shard_map/all_gather | solution.py:15
  543.8 6.3 %while.14 = (s32[]{:T(128)}, f32[2048]{0:T(1024)S(1)}, s32[]{:T(128)}, f32[8,2048]{1,0:T(8,128)}, f32[8,2048]{1,0:T(8,128)S(1)}, /*index=5*/s32[]{:T(128)}, s32[]{:T(128)}) while((s32[]{:T(128)}, f32[2048]{0:T(1024)S(1)}, s32[]{:T(128)}, f32[8,2048]{1,0:T(8,128)}, f32[8,2048]{1,0:T(8,128)S(1)}, /*index=5*/s32[]{:T(128)}, ...), condition=%wide.region_1.2_spmd.clone, body=%wide.region_0.1_spmd.clone.sunk | while | flops 8196 | bytes 65645 | solution.py:24
  550.2 6.9 %multiply_convert_fusion = bf16[512,2048]{1,0:T(8,128)(2,1)} fusion(f32[512,2048]{1,0:T(8,128)} %pad.71, f32[512,2048]{1,0:T(8,128)} %pad.72, bf16[512,2048]{1,0:T(8,128)(2,1)} %param.18, f32[2048]{0:T(1024)S(1)} %get-tuple-element.96, f32[512]{0:T(512)S(1)} %copy-done.28, f32[2048]{0:T(1024)S(1)} %copy-done.24, f32[2048]{0:T(1024)S(1)} %copy-done.23), kind=kLoop, calls=%fused_computation.7 | loop fusion | flops 8388608 | bytes 12609536 | tf_op jit(solution)/shard_map/convert_element_type | solution.py:66
  (160 shorter events, 55.2 us)
Async XLA Ops:
  7.2 7.2 %copy-start.8 = (f32[128,2048]{1,0:T(8,128)S(1)}, f32[128,2048]{1,0:T(8,128)}, u32[]{:S(2)}) copy-start(f32[128,2048]{1,0:T(8,128)} %param.16) | copy-start | bytes 3145732
  7.2 217.6 %all-gather.5.cloned.1.call-start = ((), (), s32[]{:S(2)}) async-start(), calls=%async_computation | async-start | bytes 10485760 | tf_op jit(solution)/shard_map/all_gather | solution.py:49
  11.2 8.3 %collective-permute-start = (bf16[127,2048]{1,0:T(8,128)(2,1)}, bf16[127,2048]{1,0:T(8,128)(2,1)}, u32[]{:S(2)}, u32[]{:S(2)}) collective-permute-start(bf16[127,2048]{1,0:T(8,128)(2,1)} %slice.256), channel_id=1, source_target_pairs={{0,4},{4,8},{8,12},{12,16},{16,20},{20,24},{24,28},{1,5},{5,9},{9,... | collective-permute-start | bytes 1560584 | tf_op jit(solution)/shard_map/ppermute | solution.py:10
  21.4 45.6 %copy-start.7 = (bf16[512,2048]{1,0:T(8,128)(2,1)S(1)}, bf16[512,2048]{1,0:T(8,128)(2,1)}, u32[]{:S(2)}) copy-start(bf16[512,2048]{1,0:T(8,128)(2,1)} %param.13) | copy-start | bytes 6291460
  69.9 315.7 %all-gather.7.cloned.1.call-start = ((), (), s32[]{:S(2)}) async-start(), calls=%async_computation.1 | async-start | bytes 37748736 | tf_op jit(solution)/shard_map/all_gather | solution.py:50
  71.3 369.6 %copy-start.12 = (f32[2048]{0:T(1024)}, f32[2048]{0:T(1024)S(1)}, u32[]{:S(2)}) copy-start(f32[2048]{0:T(1024)S(1)} %get-tuple-element.138) | copy-start | bytes 24580
  71.3 377.9 %copy-start.14 = (f32[2048]{0:T(1024)}, f32[2048]{0:T(1024)S(1)}, u32[]{:S(2)}) copy-start(f32[2048]{0:T(1024)S(1)} %get-tuple-element.141) | copy-start | bytes 24580
  71.3 384.2 %copy-start.16 = (f32[2048]{0:T(1024)}, f32[2048]{0:T(1024)S(1)}, u32[]{:S(2)}) copy-start(f32[2048]{0:T(1024)S(1)} %get-tuple-element.140) | copy-start | bytes 24580
  71.3 389.7 %copy-start.18 = (f32[2048]{0:T(1024)}, f32[2048]{0:T(1024)S(1)}, u32[]{:S(2)}) copy-start(f32[2048]{0:T(1024)S(1)} %get-tuple-element.132) | copy-start | bytes 24580
  71.4 392.9 %copy-start.20 = (f32[2048]{0:T(1024)}, f32[2048]{0:T(1024)S(1)}, u32[]{:S(2)}) copy-start(f32[2048]{0:T(1024)S(1)} %get-tuple-element.133) | copy-start | bytes 24580
  443.5 39.1 %copy-start.1 = (f32[256,2048]{1,0:T(8,128)}, f32[256,2048]{1,0:T(8,128)S(1)}, u32[]{:S(2)}) copy-start(f32[256,2048]{1,0:T(8,128)S(1)} %multiply_add_fusion) | copy-start | bytes 6291460
  450.9 28.6 %copy-start.5 = (f32[128,2048]{1,0:T(8,128)}, f32[128,2048]{1,0:T(8,128)S(1)}, u32[]{:S(2)}) copy-start(f32[128,2048]{1,0:T(8,128)S(1)} %multiply_add_fusion.1) | copy-start | bytes 3145732
  468.0 19.3 %slice-start.3 = ((f32[8,2048]{1,0:T(8,128)}), f32[1,2048]{1,0:T(1,128)S(1)}, s32[]{:S(2)}) async-start(f32[8,2048]{1,0:T(8,128)} %multiply_add_fusion.5), calls=%async_computation.5 | async-start | bytes 16384 | tf_op jit(solution)/shard_map/slice | solution.py:56
  477.8 9.8 %copy-start.10 = (f32[15,2048]{1,0:T(8,128)S(1)}, f32[15,2048]{1,0:T(8,128)}, u32[]{:S(2)}) copy-start(f32[15,2048]{1,0:T(8,128)} %slice.246) | copy-start | bytes 368644
  479.5 7.9 %copy-start.11 = (f32[7,2048]{1,0:T(8,128)S(1)}, f32[7,2048]{1,0:T(8,128)}, u32[]{:S(2)}) copy-start(f32[7,2048]{1,0:T(8,128)} %slice.244) | copy-start | bytes 172036
  479.6 7.9 %copy-start.22 = (f32[2048]{0:T(1024)S(1)}, f32[2048]{0:T(1024)}, u32[]{:S(2)}) copy-start(f32[2048]{0:T(1024)} %get-tuple-element.135) | copy-start | bytes 24580
  479.6 7.9 %copy-start.27 = (f32[1,2048]{1,0:T(1,128)S(1)}, f32[1,2048]{1,0:T(1,128)}, u32[]{:S(2)}) copy-start(f32[1,2048]{1,0:T(1,128)} %slice.262) | copy-start | bytes 24580
  479.6 8.0 %copy-start.21 = (f32[2048]{0:T(1024)S(1)}, f32[2048]{0:T(1024)}, u32[]{:S(2)}) copy-start(f32[2048]{0:T(1024)} %copy-done.20) | copy-start | bytes 24580
  479.6 8.0 %copy-start.26 = (f32[1,2048]{1,0:T(1,128)S(1)}, f32[1,2048]{1,0:T(1,128)}, u32[]{:S(2)}) copy-start(f32[1,2048]{1,0:T(1,128)} %slice.261) | copy-start | bytes 24580
  490.2 5.3 copy-start.15
  507.9 16.7 %copy-start.3 = (f32[256,2048]{1,0:T(8,128)S(1)}, f32[256,2048]{1,0:T(8,128)}, u32[]{:S(2)}) copy-start(f32[256,2048]{1,0:T(8,128)} %add.183) | copy-start | bytes 6291460
  524.6 25.5 %copy-start.23 = (f32[2048]{0:T(1024)S(1)}, f32[2048]{0:T(1024)}, u32[]{:S(2)}) copy-start(f32[2048]{0:T(1024)} %get-tuple-element.131) | copy-start | bytes 24580
  524.7 25.5 %copy-start.24 = (f32[2048]{0:T(1024)S(1)}, f32[2048]{0:T(1024)}, u32[]{:S(2)}) copy-start(f32[2048]{0:T(1024)} %get-tuple-element.142) | copy-start | bytes 24580
  524.7 25.5 %copy-start.28 = (f32[512]{0:T(512)S(1)}, f32[512]{0:T(512)}, u32[]{:S(2)}) copy-start(f32[512]{0:T(512)} %iota_add_fusion) | copy-start | bytes 6148
  (14 other events, 22.9 us)
Sparse Core Ops, SparseCore 0:
  70.0 154.7 all-gather.4
  226.6 158.9 all-gather.6
where the time goes:
time: 566 us; the launch traced here: 564 us
  waiting for transfers between devices  300 us (53%)
  local copies, waits for them, and re-layouts  111 us (20%)
  matrix products  71.2 us (13%)
  other arithmetic  40.3 us (7%)
  blocking collectives  23.3 us (4%)
  between operations  14.7 us (3%)
    all_gather x1, waiting for transfers between devices, body(): all_rows = lax.all_gather(mr_out, 'ctx', axis=0, tiled=True)  161 us
    all_gather x1, waiting for transfers between devices, body(): gathered = lax.all_gather(gated, 'mp', axis=1, tiled=True)  138 us
    slice x34, local copies, waits for them, and re-layouts, body(): lax.associative_scan(link_pair, (decay_rows, drive_li), axis=0)  61.5 us
    conv_general_dilated x1, matrix products, body(): lax.conv_general_dilated(padded, kernel, (1,), 'VALID', dimension_numbers...  45.6 us
    pad x16, local copies, waits for them, and re-layouts, body(): lax.associative_scan(link_pair, (decay_rows, drive_li), axis=0)  35.5 us
    dot_general x1, matrix products, body(): summed = jnp.dot(gathered, all_rows, preferred_element_type=jnp.float32)  25.6 us
    all_gather x2, blocking collectives, carried_in(): pieces = jax.tree.map(lambda part: lax.all_gather(part, axis), value)  23.3 us
    add x16, other arithmetic, link_pair(): return (earlier[0] * later[0], later[0] * earlier[1] + later[1])  16.2 us
  transfers between devices with their start and end apart: 3, of which 2 were waited for; matrix products, arithmetic and copies ran while one was open for 1% of the time, Pallas kernels for 0%

commit v1 on v0

--- a/solution.py
+++ b/solution.py
@@ -2,6 +2,12 @@
 import jax.numpy as jnp
 from jax import lax
 from jax.sharding import PartitionSpec as P
+
+
+def point_ways(local_block, axis_no):
+    r_now = list(local_block.shape[1:])
+    r_now[axis_no] *= local_block.shape[0]
+    return jnp.moveaxis(local_block, 0, axis_no).reshape(r_now)
 
 
 def passed_along(value, axis, by):
@@ -46,7 +52,29 @@
         precision=lax.Precision.HIGHEST,
     )[0]
     gated = (q_mr.astype(jnp.float32) * filtered).astype(jnp.bfloat16)
-    gathered = lax.all_gather(gated, "mp", axis=1, tiled=True)
+    lanes = jax.lax.psum(1, axis_name="mp")
+    by_rank = []
+    for hop_no in tuple(range(lanes)):
+        by_rank.append((hop_no, (hop_no + 1) % lanes))
+    bank = []
+    for at, p in by_rank:
+        bank.append((p, at))
+    f_now, view_out = ([], [])
+    for ii in tuple(range(lanes - 1)):
+        if ii % 2 == 0:
+            answer = jax.lax.ppermute(f_now[-1] if f_now else gated, axis_name="mp", perm=by_rank)
+            f_now.append(answer)
+        else:
+            long_array = jax.lax.ppermute(
+                view_out[-1] if view_out else gated, axis_name="mp", perm=bank
+            )
+            view_out.append(long_array)
+    front = jnp.stack([*f_now[::-1], gated, *view_out], 0)
+    passed = len(f_now)
+    w_next = jax.lax.axis_index("mp")
+    k_now = w_next - passed
+    front = front[(jnp.arange(lanes) - k_now) % lanes]
+    gathered = point_ways(front, 1)
     all_rows = lax.all_gather(mr_out, "ctx", axis=0, tiled=True)
     summed = jnp.dot(gathered, all_rows, preferred_element_type=jnp.float32)
     mixed = (resid_in.astype(jnp.float32) + summed).astype(jnp.bfloat16)

time: 566 us -> 426 us (0.75)
  waiting for transfers between devices: 300 us -> 78.2 us
  blocking collectives: 23.3 us -> 67.5 us
  local copies, waits for them, and re-layouts: 111 us -> 135 us
  other arithmetic: 40.3 us -> 49.2 us
    all_gather x1, waiting for transfers between devices: 161 us -> 0.01 us  [body(): all_rows = lax.all_gather(mr_out, 'ctx', axis=0, tiled=True)]
    all_gather x1 -> x0, waiting for transfers between devices: 138 us -> none  [body(): gathered = lax.all_gather(gated, 'mp', axis=1, tiled=True)]
    ppermute x0 -> x3, waiting for transfers between devices: none -> 77.5 us  [the longest x2 77.5 us: body(): jax.lax.ppermute(f_now[-1] if f_now else gated, axis_name='mp', perm=by_r...]
    all_gather x2, blocking collectives: 23.3 us -> 67.5 us  [carried_in(): pieces = jax.tree.map(lambda part: lax.all_gather(part, axis), value)]
    gather x0 -> x3, local copies, waits for them, and re-layouts: none -> 13.8 us  [body(): front = front[(jnp.arange(lanes) - k_now) % lanes]]
    transpose x0 -> x1, local copies, waits for them, and re-layouts: none -> 11.5 us  [point_ways(): return jnp.moveaxis(local_block, 0, axis_no).reshape(r_now)]
    transpose x0 -> x1, other arithmetic: none -> 8.19 us  [point_ways(): return jnp.moveaxis(local_block, 0, axis_no).reshape(r_now)]
  transfers between devices with their start and end apart: 3 -> 5, of which waited for: 2 -> 2; matrix products, arithmetic and copies ran while one was open for 1% -> 23% of each run, Pallas kernels for 0% -> 0%
where the time goes in v1:
time: 426 us; the launch traced here: 424 us
  local copies, waits for them, and re-layouts  135 us (32%)
  waiting for transfers between devices  78.2 us (18%)
  matrix products  71 us (17%)
  blocking collectives  67.5 us (16%)
  other arithmetic  49.2 us (12%)
  between operations  14.8 us (3%)
  starting transfers between devices  7.84 us (2%)
    ppermute x2, waiting for transfers between devices, body(): jax.lax.ppermute(f_now[-1] if f_now else gated, axis_name='mp', perm=by_r...  77.5 us
    all_gather x2, blocking collectives, carried_in(): pieces = jax.tree.map(lambda part: lax.all_gather(part, axis), value)  67.5 us
    slice x34, local copies, waits for them, and re-layouts, body(): lax.associative_scan(link_pair, (decay_rows, drive_li), axis=0)  61 us
    conv_general_dilated x1, matrix products, body(): lax.conv_general_dilated(padded, kernel, (1,), 'VALID', dimension_numbers...  45.6 us
    pad x16, local copies, waits for them, and re-layouts, body(): lax.associative_scan(link_pair, (decay_rows, drive_li), axis=0)  35.2 us
    dot_general x1, matrix products, body(): summed = jnp.dot(gathered, all_rows, preferred_element_type=jnp.float32)  25.4 us
    add x16, other arithmetic, link_pair(): return (earlier[0] * later[0], later[0] * earlier[1] + later[1])  15.7 us
    gather x3, local copies, waits for them, and re-layouts, body(): front = front[(jnp.arange(lanes) - k_now) % lanes]  13.8 us
  transfers between devices with their start and end apart: 5, of which 2 were waited for; matrix products, arithmetic and copies ran while one was open for 23% of the time, Pallas kernels for 0%

profile of v1, /device:TPU:0, one launch (start us, length us, event | category | flops | bytes accessed | tf_op | source)
XLA Modules:
  0.0 423.8 jit_solution(3130670643961963972)
XLA Ops:
  15.1 5.2 %rev.3 = f32[128,2048]{1,0:T(8,128)} reverse(f32[128,2048]{1,0:T(8,128)S(1)} %copy-done.4), dimensions={0} | reverse | bytes 2097152 | tf_op jit(solution)/shard_map/rev | solution.py:44
  22.2 45.6 %fusion = f32[1,512,2048]{2,0,1:T(1,128)S(1)} fusion(bf16[1,639,2048]{2,1,0:T(8,128)(2,1)S(1)} %maximum_bitcast_fusion.1, f32[128,1,2048]{2,0,1:T(8,128)S(1)} %bitcast.33), kind=kOutput, calls=%fused_computation.7 | convolution fusion | flops 1610612736 | bytes 7860224 | tf_op jit(solution)/shard_map/conv_general_dilated | solution.py:45
  74.8 45.4 %collective-permute-done.1 = bf16[512,2048]{1,0:T(8,128)(2,1)} collective-permute-done((bf16[512,2048]{1,0:T(8,128)(2,1)S(1)}, bf16[512,2048]{1,0:T(8,128)(2,1)}, u32[]{:S(2)}, u32[]{:S(2)}) %collective-permute-start.1) | collective-permute-done | bytes 2097184 | tf_op jit(solution)/shard_map/ppermute | solution.py:65
  120.9 54.5 %all-gather = f32[16384]{0:T(1024)S(1)} all-gather(f32[2048]{0:T(1024)S(1)} %get-tuple-element.141), channel_id=2, replica_groups=mesh['ctx'=8,'mp'=4] {'ctx'}, dimensions={0}, use_global_device_ids=true | all-gather | bytes 73728 | tf_op jit(solution)/shard_map/all_gather | solution.py:21
  176.7 32.1 %collective-permute-done.2 = bf16[512,2048]{1,0:T(8,128)(2,1)} collective-permute-done((bf16[512,2048]{1,0:T(8,128)(2,1)}, bf16[512,2048]{1,0:T(8,128)(2,1)}, u32[]{:S(2)}, u32[]{:S(2)}) %collective-permute-start.2) | collective-permute-done | bytes 2097184 | tf_op jit(solution)/shard_map/ppermute | solution.py:65
  208.8 3.8 pad_maximum_fusion
  212.6 3.8 fusion.18
  216.4 5.0 %gather_fusion = bf16[4,512,1024]{2,1,0:T(8,128)(2,1)} fusion(bf16[4,512,1024]{2,1,0:T(8,128)(2,1)} %get-tuple-element.127, s32[1024]{0:T(1024)S(1)} %pad_clamp_fusion), kind=kCustom, calls=%fused_computation | custom fusion | bytes 8388624 | tf_op jit(solution)/shard_map/gather | solution.py:76
  221.4 5.0 %gather_fusion.1 = bf16[4,512,1024]{2,1,0:T(8,128)(2,1)} fusion(bf16[4,512,1024]{2,1,0:T(8,128)(2,1)} %get-tuple-element.128, s32[1024]{0:T(1024)S(1)} %pad_clamp_fusion), kind=kCustom, calls=%fused_computation.1 | custom fusion | bytes 8388624 | tf_op jit(solution)/shard_map/gather | solution.py:76
  226.4 8.2 %maximum_bitcast_fusion = bf16[512,4,2048]{2,0,1:T(8,128)(2,1)} fusion(bf16[4,512,1024]{2,1,0:T(8,128)(2,1)} %gather_fusion.1, bf16[4,512,1024]{2,1,0:T(8,128)(2,1)} %gather_fusion), kind=kLoop, calls=%fused_computation.6 | loop fusion | flops 16777216 | bytes 16777216 | tf_op jit(solution)/shard_map/transpose | solution.py:10
  234.6 11.5 %copy.18 = bf16[512,4,2048]{0,2,1:T(8,128)(2,1)} copy(bf16[512,4,2048]{2,0,1:T(8,128)(2,1)} %maximum_bitcast_fusion) | data formatting | bytes 16777216 | tf_op jit(solution)/shard_map/transpose | solution.py:10
  246.1 25.4 %convert_multiply_fusion = (f32[512,2048]{1,0:T(8,128)}, bf16[512,2048]{1,0:T(8,128)(2,1)}) fusion(bf16[512,2048]{1,0:T(8,128)(2,1)S(1)} %copy-done.33, bf16[512,8192]{0,1:T(8,128)(2,1)} %bitcast.31, bf16[8192,2048]{1,0:T(8,128)(2,1)} %all-gather.4.cloned.1.call-done, bf16[512,2048]{1,0:T(8,128)(2,1)} %param.12), kind=kOutput, calls=%fused_computation.12 | convolution fusion | flops 17186160640 | bytes 52428800 | tf_op jit(solution)/shard_map/dot_general | solution.py:79
  271.6 9.8 %slice.199 = f32[256,2048]{1,0:T(8,128)} slice(f32[512,2048]{1,0:T(8,128)} %get-tuple-element.145), slice={[0:511:2], [0:2048:1]} | slice | bytes 4194304 | tf_op jit(solution)/shard_map/slice | solution.py:84
  281.4 9.8 %slice.200 = f32[256,2048]{1,0:T(8,128)} slice(f32[512,2048]{1,0:T(8,128)} %get-tuple-element.145), slice={[1:512:2], [0:2048:1]} | slice | bytes 4194304 | tf_op jit(solution)/shard_map/slice | solution.py:84
  293.7 3.3 slice.204
  332.4 10.1 %slice.254 = f32[255,2048]{1,0:T(8,128)} slice(f32[512,2048]{1,0:T(8,128)} %get-tuple-element.145), slice={[2:512:2], [0:2048:1]} | slice | bytes 4177920 | tf_op jit(solution)/shard_map/slice | solution.py:84
  348.9 4.2 pad.69
  353.1 4.8 %pad.70 = f32[256,2048]{1,0:T(8,128)} pad(f32[128,2048]{1,0:T(8,128)S(1)} %add.207, f32[]{:T(128)} %constant.58.clone.1), padding=1_0_1x0_0_0 | pad | bytes 3145732 | tf_op jit(solution)/shard_map/pad | solution.py:84
  357.9 3.2 add.209
  361.1 16.5 %pad.72 = f32[512,2048]{1,0:T(8,128)} pad(f32[256,2048]{1,0:T(8,128)} %add.209, f32[]{:T(128)} %constant.58.clone.1), padding=1_0_1x0_0_0 | pad | bytes 6291460 | tf_op jit(solution)/shard_map/pad | solution.py:84
  380.8 9.0 %pad.71 = f32[512,2048]{1,0:T(8,128)} pad(f32[256,2048]{1,0:T(8,128)S(1)} %pad_maximum_fusion.1, f32[]{:T(128)} %constant.58.clone.1), padding=0_1_1x0_0_0 | pad | bytes 6291460 | tf_op jit(solution)/shard_map/pad | solution.py:84
  390.7 13.0 %all-gather.1 = f32[8,1,2048]{2,1,0:T(1,128)S(1)} all-gather(f32[1,1,2048]{2,1,0:T(1,128)S(1)} %add_bitcast_fusion), channel_id=1, replica_groups=mesh['ctx'=8,'mp'=4] {'ctx'}, dimensions={0}, use_global_device_ids=true | all-gather | bytes 73728 | tf_op jit(solution)/shard_map/all_gather | solution.py:21
  403.7 6.3 %while.14 = (s32[]{:T(128)}, f32[2048]{0:T(1024)S(1)}, s32[]{:T(128)}, f32[8,2048]{1,0:T(8,128)}, f32[8,2048]{1,0:T(8,128)S(1)}, /*index=5*/s32[]{:T(128)}, s32[]{:T(128)}) while((s32[]{:T(128)}, f32[2048]{0:T(1024)S(1)}, s32[]{:T(128)}, f32[8,2048]{1,0:T(8,128)}, f32[8,2048]{1,0:T(8,128)S(1)}, /*index=5*/s32[]{:T(128)}, ...), condition=%wide.region_1.2_spmd.clone, body=%wide.region_0.1_spmd.clone.sunk | while | flops 8196 | bytes 65637 | solution.py:30
  410.0 6.9 %multiply_convert_fusion = bf16[512,2048]{1,0:T(8,128)(2,1)} fusion(f32[512,2048]{1,0:T(8,128)} %pad.71, f32[512,2048]{1,0:T(8,128)} %pad.72, bf16[512,2048]{1,0:T(8,128)(2,1)} %param.18, f32[2048]{0:T(1024)S(1)} %get-tuple-element.96, f32[512]{0:T(512)S(1)} %copy-done.30, f32[2048]{0:T(1024)S(1)} %copy-done.25, f32[2048]{0:T(1024)S(1)} %copy-done.24), kind=kLoop, calls=%fused_computation.11 | loop fusion | flops 8388608 | bytes 12609536 | tf_op jit(solution)/shard_map/convert_element_type | solution.py:94
  (177 shorter events, 72.6 us)
Async XLA Ops:
  7.2 239.0 %all-gather.4.cloned.1.call-start = ((), (), s32[]{:S(2)}) async-start(), calls=%async_computation | async-start | bytes 37748736 | tf_op jit(solution)/shard_map/all_gather | solution.py:78
  11.9 8.4 %collective-permute-start = (bf16[127,2048]{1,0:T(8,128)(2,1)}, bf16[127,2048]{1,0:T(8,128)(2,1)}, u32[]{:S(2)}, u32[]{:S(2)}) collective-permute-start(bf16[127,2048]{1,0:T(8,128)(2,1)} %slice.260), channel_id=1, source_target_pairs={{0,4},{4,8},{8,12},{12,16},{16,20},{20,24},{24,28},{1,5},{5,9},{9,... | collective-permute-start | bytes 1560584 | tf_op jit(solution)/shard_map/ppermute | solution.py:16
  22.2 45.6 %copy-start.3 = (bf16[512,2048]{1,0:T(8,128)(2,1)S(1)}, bf16[512,2048]{1,0:T(8,128)(2,1)}, u32[]{:S(2)}) copy-start(bf16[512,2048]{1,0:T(8,128)(2,1)} %param.13) | copy-start | bytes 6291460
  67.8 52.4 %copy-start.31 = (f32[2048]{0:T(1024)S(1)}, f32[2048]{0:T(1024)}, u32[]{:S(2)}) copy-start(f32[2048]{0:T(1024)} %param.21) | copy-start | bytes 24580
  67.8 52.4 %copy-start.32 = (f32[2048]{0:T(1024)S(1)}, f32[2048]{0:T(1024)}, u32[]{:S(2)}) copy-start(f32[2048]{0:T(1024)} %param.20) | copy-start | bytes 24580
  70.2 50.0 %collective-permute-start.1 = (bf16[512,2048]{1,0:T(8,128)(2,1)S(1)}, bf16[512,2048]{1,0:T(8,128)(2,1)}, u32[]{:S(2)}, u32[]{:S(2)}) collective-permute-start(bf16[512,2048]{1,0:T(8,128)(2,1)S(1)} %fusion.2), channel_id=1, source_target_pairs={{0,1},{1,2},{2,3},{3,0},{4,5},{5,6},{6,7},{7,4},{8,9},{9,10},{10,1... | collective-permute-start | bytes 6291464 | tf_op jit(solution)/shard_map/ppermute | solution.py:65
  72.7 104.0 %collective-permute-start.3 = (bf16[512,2048]{1,0:T(8,128)(2,1)S(1)}, bf16[512,2048]{1,0:T(8,128)(2,1)}, u32[]{:S(2)}, u32[]{:S(2)}) collective-permute-start(bf16[512,2048]{1,0:T(8,128)(2,1)S(1)} %fusion.2), channel_id=1, source_target_pairs={{1,0},{2,1},{3,2},{0,3},{5,4},{6,5},{7,6},{4,7},{9,8},{10,9},{11,1... | collective-permute-start | bytes 6291464 | tf_op jit(solution)/shard_map/ppermute | solution.py:68
  120.2 88.6 %collective-permute-start.2 = (bf16[512,2048]{1,0:T(8,128)(2,1)}, bf16[512,2048]{1,0:T(8,128)(2,1)}, u32[]{:S(2)}, u32[]{:S(2)}) collective-permute-start(bf16[512,2048]{1,0:T(8,128)(2,1)} %collective-permute-done.1), channel_id=1, source_target_pairs={{0,1},{1,2},{2,3},{3,0},{4,5},{5,6},{6,7},{7,4},{8,9},{9,10},{10,1... | collective-permute-start | bytes 6291464 | tf_op jit(solution)/shard_map/ppermute | solution.py:65
  120.9 170.3 %copy-start.9 = (f32[2048]{0:T(1024)}, f32[2048]{0:T(1024)S(1)}, u32[]{:S(2)}) copy-start(f32[2048]{0:T(1024)S(1)} %get-tuple-element.140) | copy-start | bytes 24580
  120.9 179.0 %copy-start.11 = (f32[2048]{0:T(1024)}, f32[2048]{0:T(1024)S(1)}, u32[]{:S(2)}) copy-start(f32[2048]{0:T(1024)S(1)} %get-tuple-element.143) | copy-start | bytes 24580
  120.9 183.7 %copy-start.13 = (f32[2048]{0:T(1024)}, f32[2048]{0:T(1024)S(1)}, u32[]{:S(2)}) copy-start(f32[2048]{0:T(1024)S(1)} %get-tuple-element.142) | copy-start | bytes 24580
  120.9 189.1 %copy-start.15 = (f32[2048]{0:T(1024)}, f32[2048]{0:T(1024)S(1)}, u32[]{:S(2)}) copy-start(f32[2048]{0:T(1024)S(1)} %get-tuple-element.134) | copy-start | bytes 24580
  120.9 191.6 %copy-start.17 = (f32[2048]{0:T(1024)}, f32[2048]{0:T(1024)S(1)}, u32[]{:S(2)}) copy-start(f32[2048]{0:T(1024)S(1)} %get-tuple-element.135) | copy-start | bytes 24580
  293.7 38.7 %copy-start = (f32[256,2048]{1,0:T(8,128)}, f32[256,2048]{1,0:T(8,128)S(1)}, u32[]{:S(2)}) copy-start(f32[256,2048]{1,0:T(8,128)S(1)} %multiply_add_fusion) | copy-start | bytes 6291460
  301.5 27.8 %copy-start.1 = (f32[128,2048]{1,0:T(8,128)}, f32[128,2048]{1,0:T(8,128)S(1)}, u32[]{:S(2)}) copy-start(f32[128,2048]{1,0:T(8,128)S(1)} %multiply_add_fusion.1) | copy-start | bytes 3145732
  326.7 17.6 %slice-start.3 = ((f32[8,2048]{1,0:T(8,128)}), f32[1,2048]{1,0:T(1,128)S(1)}, s32[]{:S(2)}) async-start(f32[8,2048]{1,0:T(8,128)} %multiply_add_fusion.5), calls=%async_computation.4 | async-start | bytes 16384 | tf_op jit(solution)/shard_map/slice | solution.py:84
  329.4 15.0 %copy-start.6 = (f32[7,2048]{1,0:T(8,128)S(1)}, f32[7,2048]{1,0:T(8,128)}, u32[]{:S(2)}) copy-start(f32[7,2048]{1,0:T(8,128)} %slice.244) | copy-start | bytes 172036
  329.4 15.0 %copy-start.19 = (f32[2048]{0:T(1024)S(1)}, f32[2048]{0:T(1024)}, u32[]{:S(2)}) copy-start(f32[2048]{0:T(1024)} %get-tuple-element.137) | copy-start | bytes 24580
  329.4 15.0 %copy-start.29 = (f32[1,2048]{1,0:T(1,128)S(1)}, f32[1,2048]{1,0:T(1,128)}, u32[]{:S(2)}) copy-start(f32[1,2048]{1,0:T(1,128)} %slice.266) | copy-start | bytes 24580
  329.4 15.1 %copy-start.18 = (f32[2048]{0:T(1024)S(1)}, f32[2048]{0:T(1024)}, u32[]{:S(2)}) copy-start(f32[2048]{0:T(1024)} %copy-done.17) | copy-start | bytes 24580
  361.1 16.5 %copy-start.10 = (f32[2048]{0:T(1024)S(1)}, f32[2048]{0:T(1024)}, u32[]{:S(2)}) copy-start(f32[2048]{0:T(1024)} %copy-done.9) | copy-start | bytes 24580
  380.7 29.3 %copy-start.24 = (f32[2048]{0:T(1024)S(1)}, f32[2048]{0:T(1024)}, u32[]{:S(2)}) copy-start(f32[2048]{0:T(1024)} %get-tuple-element.133) | copy-start | bytes 24580
  380.7 29.3 %copy-start.25 = (f32[2048]{0:T(1024)S(1)}, f32[2048]{0:T(1024)}, u32[]{:S(2)}) copy-start(f32[2048]{0:T(1024)} %get-tuple-element.144) | copy-start | bytes 24580
  380.7 29.3 %copy-start.30 = (f32[512]{0:T(512)S(1)}, f32[512]{0:T(512)}, u32[]{:S(2)}) copy-start(f32[512]{0:T(512)} %iota_add_fusion) | copy-start | bytes 6148
  (19 other events, 168.9 us)
Sparse Core Ops, SparseCore 0:
  9.9 163.5 all-gather.3
